TPU v7x, 256 devices: a whole 4x4x8 slice. The times are simulated.
256 devices in a mesh: lat: 16 (over x_lo, y, core), lon: 16 (over x_hi, z).
Axes of the slice: x: 4 (x_hi: 2, x_lo: 2; x = x_hi * 2 + x_lo), y: 4, z: 8, core: 2. Of those that a mesh axis runs over, the one named last changes fastest.
Arguments:
- tokens: bfloat16 [2, 96, 192, 1024], P(None, 'lat', 'lon'), may hold values from -6 to 6
- layer_norm_gain: float32 [1024], replicated, may hold values from 0.5 to 1.5
- layer_norm_bias: float32 [1024], replicated, may hold values from -3 to 3
- w_qkv: bfloat16 [1024, 1536], replicated, may hold values from -2 to 2
- w_out: bfloat16 [512, 1024], replicated, may hold values from -0.25 to 0.25
- output_cotangent: bfloat16 [2, 96, 192, 1024], P(None, 'lat', 'lon'), may hold values from -6 to 6
Outputs:
- output: bfloat16 [2, 96, 192, 1024], P(None, 'lat', 'lon')
- token_gradient: bfloat16 [2, 96, 192, 1024], P(None, 'lat', 'lon')
- d_qkv: float32 [1024, 1536], P(('lat', 'lon'))
- d_out: float32 [512, 1024], P(None, ('lat', 'lon'))
- gain_gradient_scaled: float32 [1024], P(('lat', 'lon'))
- d_bias: float32 [1024], P(('lat', 'lon'))
All inputs are finite; a program needn't handle non-finite values.
Results may differ from a plain program's by a relative error of at most 0.0093.
Values may be sent and summed in bfloat16 or wider, within the bound.
A program may use at most 64 MiB of HBM per device.

v0:
```python
import math

import jax
import jax.numpy as jnp
from jax import lax
from jax.sharding import PartitionSpec as P

HDIM = 64
WLAT = 6
WLON = 12


def padded(cells, sides, width):
    for axis, dim in sides:
        count = lax.axis_size(axis)
        ends = count - 1
        head = lax.slice_in_dim(cells, 0, width, axis=dim)
        tail = lax.slice_in_dim(cells, cells.shape[dim] - width, cells.shape[dim], axis=dim)
        cells = jnp.concatenate(
            [
                lax.ppermute(tail, axis, [(i, (i + 1) % count) for i in range(ends)]),
                cells,
                lax.ppermute(head, axis, [((i + 1) % count, i) for i in range(ends)]),
            ],
            axis=dim,
        )
    return cells


def windows(grid_data, win_rows):
    levels, row_total, col_total, channels = grid_data.shape
    grid_data = grid_data.reshape(
        levels, row_total // win_rows, win_rows, col_total // WLON, WLON, channels
    )
    grid_data = grid_data.transpose(1, 3, 0, 2, 4, 5)
    return grid_data.reshape(-1, levels * win_rows * WLON, channels)


def from_windows(win_data, levels, row_total, col_total, win_rows):
    channels = win_data.shape[-1]
    grid_data = win_data.reshape(
        row_total // win_rows, col_total // WLON, levels, win_rows, WLON, channels
    )
    grid_data = grid_data.transpose(2, 0, 3, 1, 4, 5)
    return grid_data.reshape(levels, row_total, col_total, channels)


def attend(queries, key_part, value_part, grad_att, key_valid):
    score_scale = queries.shape[-1] ** (-0.5)
    scores = (
        jnp.einsum("nqhd,nkhd->nhqk", queries, key_part, preferred_element_type=jnp.float32)
        * score_scale
    )
    scores = jnp.where(key_valid[:, None, None, :], scores, -1e30)
    row_max = jnp.max(scores, axis=-1, keepdims=True)
    exp_scores = jnp.exp(scores - row_max)
    probabilities = exp_scores / jnp.sum(exp_scores, axis=-1, keepdims=True)
    probs_low = probabilities.astype(jnp.bfloat16)
    attended = jnp.einsum(
        "nhqk,nkhd->nqhd", probs_low, value_part, preferred_element_type=jnp.float32
    ).astype(jnp.bfloat16)
    grad_prob = jnp.einsum(
        "nqhd,nkhd->nhqk", grad_att, value_part, preferred_element_type=jnp.float32
    )
    row_inner = jnp.sum(probabilities * grad_prob, axis=-1, keepdims=True)
    grad_score = (probabilities * (grad_prob - row_inner)).astype(jnp.bfloat16)
    grad_query = (
        jnp.einsum("nhqk,nkhd->nqhd", grad_score, key_part, preferred_element_type=jnp.float32)
        * score_scale
    ).astype(jnp.bfloat16)
    grad_key = (
        jnp.einsum("nhqk,nqhd->nkhd", grad_score, queries, preferred_element_type=jnp.float32)
        * score_scale
    )
    grad_value = jnp.einsum(
        "nhqk,nqhd->nkhd", probs_low, grad_att, preferred_element_type=jnp.float32
    )
    return (attended, grad_query, grad_key, grad_value)


def run_windows(per_query, per_key, query_rows, key_valid):
    levels, query_total, col_total, channels = per_query.shape
    key_total = per_key.shape[1]
    inner_width = channels // 2
    head_dim = HDIM
    head_count = inner_width // head_dim
    query_win = windows(per_query, query_rows)
    key_win = windows(per_key, WLAT)
    win_count, query_len, _ = query_win.shape
    key_len = key_win.shape[1]
    attended, grad_query, grad_key, grad_value = attend(
        query_win[..., :inner_width].reshape(win_count, query_len, head_count, head_dim),
        key_win[..., :inner_width].reshape(win_count, key_len, head_count, head_dim),
        key_win[..., inner_width:].reshape(win_count, key_len, head_count, head_dim),
        query_win[..., inner_width:].reshape(win_count, query_len, head_count, head_dim),
        key_valid,
    )
    query_out = jnp.concatenate(
        [
            attended.reshape(win_count, query_len, inner_width),
            grad_query.reshape(win_count, query_len, inner_width),
        ],
        axis=-1,
    )
    key_out = jnp.concatenate(
        [
            grad_key.reshape(win_count, key_len, inner_width),
            grad_value.reshape(win_count, key_len, inner_width),
        ],
        axis=-1,
    )
    return (
        from_windows(query_out, levels, query_total, col_total, query_rows),
        from_windows(key_out, levels, key_total, col_total, WLAT),
    )


def on_device(tokens, layer_norm_gain, layer_norm_bias, w_qkv, w_out, output_cotangent):
    levels, lat_rows, lon_cols, model_width = tokens.shape
    inner_width = w_out.shape[0]
    half_lat = WLAT // 2
    half_lon = WLON // 2
    lat_count = lax.axis_size("lat")
    lat_place = lax.axis_index("lat")
    lon_count = lax.axis_size("lon")
    lon_place = lax.axis_index("lon")
    norm_factor = 1.0 / math.sqrt(levels * lat_rows * lon_cols * lat_count * lon_count)
    tokens_wide = tokens.astype(jnp.float32)
    average = jnp.mean(tokens_wide, axis=-1, keepdims=True)
    centered_input = tokens_wide - average
    inverse_deviation = lax.rsqrt(
        jnp.mean(centered_input * centered_input, axis=-1, keepdims=True) + 1e-05
    )
    standardized_input = centered_input * inverse_deviation
    normalized_tokens = (standardized_input * layer_norm_gain + layer_norm_bias).astype(
        jnp.bfloat16
    )
    flat_normed = normalized_tokens.reshape(-1, model_width)
    projected = jnp.dot(flat_normed, w_qkv, preferred_element_type=jnp.float32).astype(jnp.bfloat16)
    projected = projected.reshape(levels, lat_rows, lon_cols, 3 * inner_width)
    key_pairs = projected[..., inner_width:]
    grad_flat = output_cotangent.reshape(-1, model_width)
    grad_att = jnp.einsum("td,hd->th", grad_flat, w_out, preferred_element_type=jnp.float32).astype(
        jnp.bfloat16
    )
    grad_att = grad_att.reshape(levels, lat_rows, lon_cols, inner_width)
    widened = padded(key_pairs, (("lon", 2),), half_lon)
    extended = padded(widened, (("lat", 1),), half_lat)
    col_total = lon_cols + WLON
    query_side = jnp.concatenate([projected[..., :inner_width], grad_att], axis=-1)
    query_side = jnp.pad(query_side, ((0, 0), (0, 0), (half_lon, half_lon), (0, 0)))
    col_ids = jnp.arange(col_total)
    left_ok = jnp.logical_or(lon_place > 0, col_ids >= half_lon)
    right_ok = jnp.logical_or(lon_place < lon_count - 1, col_ids < lon_cols + half_lon)
    col_ok = jnp.logical_and(left_ok, right_ok).astype(jnp.float32).reshape(1, 1, col_total, 1)
    row_ids = jnp.arange(WLAT)
    top_ok = jnp.logical_or(lat_place > 0, row_ids >= half_lat)
    bottom_ok = jnp.logical_or(lat_place < lat_count - 1, row_ids < half_lat)
    edge_rows = jnp.concatenate([top_ok, bottom_ok]).astype(jnp.float32)
    mask_grid = jnp.broadcast_to(
        edge_rows.reshape(1, 2 * WLAT, 1, 1) * col_ok, (levels, 2 * WLAT, col_total, 1)
    )
    edge_valid = windows(mask_grid, WLAT)[..., 0] > 0.5
    edge_query = jnp.concatenate(
        [query_side[:, :half_lat], query_side[:, lat_rows - half_lat :]], axis=1
    )
    edge_key = jnp.concatenate([extended[:, :WLAT], extended[:, lat_rows:]], axis=1)
    edge_out, edge_grads = run_windows(edge_query, edge_key, half_lat, edge_valid)
    query_results = edge_out
    query_results = query_results[:, :, half_lon : half_lon + lon_cols]
    attended = query_results[..., :inner_width]
    grad_query = query_results[..., inner_width:]
    rim_rows = jnp.concatenate(
        [edge_grads[:, :half_lat], edge_grads[:, lat_rows + half_lat :]], axis=1
    )
    received = padded(rim_rows.astype(jnp.bfloat16), (("lat", 1),), half_lat).astype(rim_rows.dtype)
    owned = edge_grads[:, half_lat : lat_rows + half_lat]
    owned = owned + jnp.pad(
        received[:, :half_lat], ((0, 0), (0, lat_rows - half_lat), (0, 0), (0, 0))
    )
    owned = owned + jnp.pad(
        received[:, 3 * half_lat :], ((0, 0), (lat_rows - half_lat, 0), (0, 0), (0, 0))
    )
    rim_cols = jnp.concatenate([owned[:, :, :half_lon], owned[:, :, lon_cols + half_lon :]], axis=2)
    received_cols = padded(rim_cols, (("lon", 2),), half_lon)
    centre = owned[:, :, half_lon : lon_cols + half_lon]
    centre = centre + jnp.pad(
        received_cols[:, :, :half_lon], ((0, 0), (0, 0), (0, lon_cols - half_lon), (0, 0))
    )
    centre = centre + jnp.pad(
        received_cols[:, :, 3 * half_lon :], ((0, 0), (0, 0), (lon_cols - half_lon, 0), (0, 0))
    )
    key_value_grads = centre.astype(jnp.bfloat16)
    grad_proj = jnp.concatenate([grad_query, key_value_grads], axis=-1).reshape(-1, 3 * inner_width)
    attended_flat = attended.reshape(-1, inner_width)
    mixed = jnp.dot(attended_flat, w_out, preferred_element_type=jnp.float32).reshape(
        tokens_wide.shape
    )
    y_out = (tokens_wide + mixed).astype(jnp.bfloat16)
    term_out = jnp.einsum("ti,td->id", attended_flat, grad_flat, preferred_element_type=jnp.float32)
    term_qkv = jnp.einsum("td,tj->dj", flat_normed, grad_proj, preferred_element_type=jnp.float32)
    gradient_of_normalized = jnp.einsum(
        "tj,dj->td", grad_proj, w_qkv, preferred_element_type=jnp.float32
    ).reshape(tokens_wide.shape)
    gain_term_value = jnp.sum(gradient_of_normalized * standardized_input, axis=(0, 1, 2))
    term_bias = jnp.sum(gradient_of_normalized, axis=(0, 1, 2))
    totals = (
        lax.psum_scatter(term_qkv, ("lat", "lon"), scatter_dimension=0, tiled=True),
        lax.psum_scatter(term_out, ("lat", "lon"), scatter_dimension=1, tiled=True),
        lax.psum_scatter(gain_term_value, ("lat", "lon"), scatter_dimension=0, tiled=True),
        lax.psum_scatter(term_bias, ("lat", "lon"), scatter_dimension=0, tiled=True),
    )
    d_qkv = totals[0] * norm_factor
    d_out = totals[1] * norm_factor
    gain_gradient_scaled = totals[2] * norm_factor
    d_bias = totals[3] * norm_factor
    gradient_of_standardized = gradient_of_normalized * layer_norm_gain
    first_moment_term = jnp.mean(gradient_of_standardized, axis=-1, keepdims=True)
    second_moment_term = jnp.mean(
        gradient_of_standardized * standardized_input, axis=-1, keepdims=True
    )
    token_gradient = (
        output_cotangent.astype(jnp.float32)
        + (gradient_of_standardized - first_moment_term - standardized_input * second_moment_term)
        * inverse_deviation
    ).astype(jnp.bfloat16)
    return (y_out, token_gradient, d_qkv, d_out, gain_gradient_scaled, d_bias)


def solution(mesh):
    in_specs = (P(None, "lat", "lon", None), P(), P(), P(), P(), P(None, "lat", "lon", None))
    out_specs = (
        P(None, "lat", "lon", None),
        P(None, "lat", "lon", None),
        P(("lat", "lon"), None),
        P(None, ("lat", "lon")),
        P(("lat", "lon")),
        P(("lat", "lon")),
    )
    return jax.shard_map(
        on_device, mesh=mesh, in_specs=in_specs, out_specs=out_specs, check_vma=False
    )
```

profile of v0, /device:TPU:32, one launch (start us, length us, event | category | flops | bytes accessed | tf_op | source)
XLA Modules:
  0.0 450.1 jit_solution(13599439648109438678)
XLA Ops:
  7.2 1.2 convert_reduce_fusion
  8.5 1.2 fusion.41
  9.7 1.3 fusion.34
  11.8 2.4 convolution_convert_fusion
  14.1 2.0 reshape.180
  16.1 1.9 fusion.62
  18.0 3.7 collective-permute-start.1
  21.8 2.1 collective-permute-start
  23.9 1.8 slice.104
  27.2 1.8 reshape.184
  29.0 2.5 convolution_convert_fusion.2
  33.8 1.4 pad_maximum_fusion
  36.1 2.1 collective-permute-start.2
  38.2 1.3 collective-permute-start.3
  40.3 1.4 gt.28
  41.6 1.3 copy.75
  43.3 1.4 copy.51
  44.8 2.8 reshape.187
  47.6 2.1 fusion.60
  49.6 2.1 copy.52
  51.7 2.0 copy.55
  53.7 1.5 fusion.17
  55.3 1.2 copy.46
  56.5 2.2 copy.47
  58.7 3.9 reshape.182
  62.7 2.7 fusion.58
  65.4 2.3 copy.48
  67.6 2.2 copy.53
  69.9 3.6 fusion.63
  73.5 3.5 fusion.12
  77.0 2.4 multiply_reduce_fusion
  79.4 2.0 convolution_bitcast_fusion.1
  81.4 3.5 copy.62
  84.9 3.2 concatenate.59
  88.1 2.8 multiply_convert_fusion
  92.0 1.7 multiply_bitcast_fusion
  93.7 3.5 copy.61
  97.2 3.1 concatenate.58
  100.4 2.9 maximum_bitcast_fusion
  103.3 1.8 copy.63
  105.1 1.7 copy.92
  106.8 2.1 copy.64
  108.9 2.6 copy.54
  111.6 2.1 concatenate.55
  113.7 1.8 fusion.57
  115.5 4.7 %collective-permute-start.4 = (bf16[2,3,24,1024]{3,2,1,0:T(8,128)(2,1)S(1)}, bf16[2,3,24,1024]{3,2,1,0:T(8,128)(2,1)}, u32[]{:S(2)}, u32[]{:S(2)}) collective-permute-start(bf16[2,3,24,1024]{3,2,1,0:T(8,128)(2,1)S(1)} %get-tuple-element.34), channel_id=1, source_target_pairs={{0,16},{16,32},{32,48},{48,64},{64,80},{80,96},{96,112},{112,128},... | collective-permute-start | bytes 884744 | tf_op jit(solution)/shard_map/ppermute | solution.py:21
  120.2 1.3 collective-permute-start.5
  121.5 2.8 fusion.13
  124.4 2.7 copy.56
  127.0 2.1 concatenate.56
  129.1 1.6 maximum_bitcast_fusion.1
  132.4 1.5 maximum_convert_fusion
  134.7 3.8 collective-permute-start.6
  138.5 2.3 collective-permute-start.7
  141.1 1.8 convolution_bitcast_fusion.2
  143.0 4.9 %collective-permute-done.6 = f32[2,6,6,1024]{3,2,1,0:T(8,128)S(1)} collective-permute-done((f32[2,6,6,1024]{3,2,1,0:T(8,128)S(1)}, f32[2,6,6,1024]{3,2,1,0:T(8,128)S(1)}, u32[]{:S(2)}, u32[]{:S(2)}) %collective-permute-start.6) | collective-permute-done | bytes 294944 | tf_op jit(solution)/shard_map/ppermute | solution.py:21
  147.9 4.9 %collective-permute-done.7 = f32[2,6,6,1024]{3,2,1,0:T(8,128)S(1)} collective-permute-done((f32[2,6,6,1024]{3,2,1,0:T(8,128)S(1)}, f32[2,6,6,1024]{3,2,1,0:T(8,128)S(1)}, u32[]{:S(2)}, u32[]{:S(2)}) %collective-permute-start.7) | collective-permute-done | bytes 294944 | tf_op jit(solution)/shard_map/ppermute | solution.py:23
  153.9 3.8 convolution_bitcast_fusion
  157.7 1.7 fusion.11
  160.5 1.4 fusion.40
  163.3 84.0 %all-reduce.8 = (f32[1024]{0:T(1024)S(1)}, f32[1024]{0:T(1024)S(1)}) all-reduce(f32[1024]{0:T(1024)S(1)} %get-tuple-element.24, f32[1024]{0:T(1024)S(1)} %get-tuple-element.27), channel_id=4, replica_groups=mesh['lat'=16,'lon'=16] {'lat','lon'}, use_global_device_ids=true, to_apply=%region_10.11.clone | all-reduce | flops 2048 | bytes 16384
  248.5 192.1 %all-reduce.12.cloned.1.call-done = (f32[1024,1536]{1,0:T(8,128)}, f32[512,1024]{0,1:T(8,128)}) async-done(((f32[1024,1536]{1,0:T(8,128)}, f32[512,1024]{0,1:T(8,128)}), (f32[1024,1536]{1,0:T(8,128)}, f32[512,1024]{0,1:T(8,128)})) %all-reduce.12.cloned.1.call-update) | async-done | bytes 8388624
  440.5 1.4 dynamic-slice_multiply_fusion
  442.0 1.3 dynamic-slice_multiply_fusion.1
  (80 shorter events, 15.1 us)
Async XLA Ops:
  7.2 4.6 %copy-start = (bf16[1024,1536]{1,0:T(8,128)(2,1)S(1)}, bf16[1024,1536]{1,0:T(8,128)(2,1)}, u32[]{:S(2)}) copy-start(bf16[1024,1536]{1,0:T(8,128)(2,1)} %param.9) | copy-start | bytes 9437188
  7.2 433.4 %all-reduce.12.cloned.1.call-start = ((), (), s32[]{:S(2)}) async-start(), calls=%async_computation | async-start | bytes 16777216
  14.1 12.3 %copy-start.5 = (bf16[2,6,12,1024]{3,0,2,1:T(2,128)(2,1)S(1)}, bf16[2,6,12,1024]{3,0,2,1:T(2,128)(2,1)}, u32[]{:S(2)}) copy-start(bf16[2,6,12,1024]{3,0,2,1:T(2,128)(2,1)} %param.11) | copy-start | bytes 884740
  18.0 15.8 %collective-permute-start.1 = (bf16[2,6,6,1024]{3,2,1,0:T(8,128)(2,1)}, bf16[2,6,6,1024]{3,2,1,0:T(8,128)(2,1)}, u32[]{:S(2)}, u32[]{:S(2)}) collective-permute-start(bf16[2,6,6,1024]{3,2,1,0:T(8,128)(2,1)} %get-tuple-element.44), channel_id=1, source_target_pairs={{1,0},{2,1},{3,2},{4,3},{5,4},{6,5},{7,6},{8,7},{9,8},{10,9},{11,1... | collective-permute-start | bytes 442376 | tf_op jit(solution)/shard_map/ppermute | solution.py:23
  21.8 12.1 %collective-permute-start = (bf16[2,6,6,1024]{3,2,1,0:T(8,128)(2,1)}, bf16[2,6,6,1024]{3,2,1,0:T(8,128)(2,1)}, u32[]{:S(2)}, u32[]{:S(2)}) collective-permute-start(bf16[2,6,6,1024]{3,2,1,0:T(8,128)(2,1)} %get-tuple-element.45), channel_id=1, source_target_pairs={{0,1},{1,2},{2,3},{3,4},{4,5},{5,6},{6,7},{7,8},{8,9},{9,10},{10,1... | collective-permute-start | bytes 442376 | tf_op jit(solution)/shard_map/ppermute | solution.py:21
  29.0 10.5 %slice-start = ((bf16[2,6,12,1536]{3,2,1,0:T(8,128)(2,1)}), bf16[2,6,12,512]{3,2,1,0:T(8,128)(2,1)S(1)}, s32[]{:S(2)}) async-start(bf16[2,6,12,1536]{3,2,1,0:T(8,128)(2,1)} %reshape.180), calls=%async_computation.1 | async-start | bytes 393216 | tf_op jit(solution)/shard_map/slice | solution.py:150
  36.1 17.7 %collective-permute-start.2 = (bf16[2,3,24,1024]{3,2,1,0:T(8,128)(2,1)}, bf16[2,3,24,1024]{3,2,1,0:T(8,128)(2,1)}, u32[]{:S(2)}, u32[]{:S(2)}) collective-permute-start(bf16[2,3,24,1024]{3,2,1,0:T(8,128)(2,1)} %get-tuple-element.42), channel_id=1, source_target_pairs={{0,16},{16,32},{32,48},{48,64},{64,80},{80,96},{96,112},{112,128},... | collective-permute-start | bytes 884744 | tf_op jit(solution)/shard_map/ppermute | solution.py:21
  38.2 15.5 %collective-permute-start.3 = (bf16[2,3,24,1024]{3,2,1,0:T(8,128)(2,1)}, bf16[2,3,24,1024]{3,2,1,0:T(8,128)(2,1)}, u32[]{:S(2)}, u32[]{:S(2)}) collective-permute-start(bf16[2,3,24,1024]{3,2,1,0:T(8,128)(2,1)} %get-tuple-element.43), channel_id=1, source_target_pairs={{16,0},{32,16},{48,32},{64,48},{80,64},{96,80},{112,96},{128,112},... | collective-permute-start | bytes 884744 | tf_op jit(solution)/shard_map/ppermute | solution.py:23
  44.8 9.0 %copy-start.4 = (bf16[2,6,12,1024]{3,2,1,0:T(8,128)(2,1)S(1)}, bf16[2,6,12,1024]{3,2,1,0:T(8,128)(2,1)}, u32[]{:S(2)}) copy-start(bf16[2,6,12,1024]{3,2,1,0:T(8,128)(2,1)} %slice.104) | copy-start | bytes 884740
  65.4 4.5 %copy-start.19 = (pred[4,144]{1,0:T(4,128)(4,1)S(1)}, pred[4,144]{1,0:T(4,128)(4,1)}, u32[]{:S(2)}) copy-start(pred[4,144]{1,0:T(4,128)(4,1)} %gt.28) | copy-start | bytes 1732
  73.5 3.5 copy-start.8
  73.5 3.5 copy-start.11
  73.5 3.5 copy-start.12
  88.1 3.9 copy-start.9
  90.9 1.1 copy-start.1
  115.5 15.8 %collective-permute-start.4 = (bf16[2,3,24,1024]{3,2,1,0:T(8,128)(2,1)S(1)}, bf16[2,3,24,1024]{3,2,1,0:T(8,128)(2,1)}, u32[]{:S(2)}, u32[]{:S(2)}) collective-permute-start(bf16[2,3,24,1024]{3,2,1,0:T(8,128)(2,1)S(1)} %get-tuple-element.34), channel_id=1, source_target_pairs={{0,16},{16,32},{32,48},{48,64},{64,80},{80,96},{96,112},{112,128},... | collective-permute-start | bytes 884744 | tf_op jit(solution)/shard_map/ppermute | solution.py:21
  120.2 11.1 %collective-permute-start.5 = (bf16[2,3,24,1024]{3,2,1,0:T(8,128)(2,1)}, bf16[2,3,24,1024]{3,2,1,0:T(8,128)(2,1)}, u32[]{:S(2)}, u32[]{:S(2)}) collective-permute-start(bf16[2,3,24,1024]{3,2,1,0:T(8,128)(2,1)} %get-tuple-element.35), channel_id=1, source_target_pairs={{16,0},{32,16},{48,32},{64,48},{80,64},{96,80},{112,96},{128,112},... | collective-permute-start | bytes 884744 | tf_op jit(solution)/shard_map/ppermute | solution.py:23
  132.3 1.9 copy-start.3
  132.3 1.9 copy-start.20
  134.6 6.5 %copy-start.6 = (bf16[2,6,12,1024]{3,0,2,1:T(2,128)(2,1)S(1)}, bf16[2,6,12,1024]{3,0,2,1:T(2,128)(2,1)}, u32[]{:S(2)}) copy-start(bf16[2,6,12,1024]{3,0,2,1:T(2,128)(2,1)} %param.11) | copy-start | bytes 884740
  134.7 13.2 %collective-permute-start.6 = (f32[2,6,6,1024]{3,2,1,0:T(8,128)S(1)}, f32[2,6,6,1024]{3,2,1,0:T(8,128)S(1)}, u32[]{:S(2)}, u32[]{:S(2)}) collective-permute-start(f32[2,6,6,1024]{3,2,1,0:T(8,128)S(1)} %get-tuple-element.32), channel_id=1, source_target_pairs={{0,1},{1,2},{2,3},{3,4},{4,5},{5,6},{6,7},{7,8},{8,9},{9,10},{10,1... | collective-permute-start | bytes 884744 | tf_op jit(solution)/shard_map/ppermute | solution.py:21
  138.5 14.3 %collective-permute-start.7 = (f32[2,6,6,1024]{3,2,1,0:T(8,128)S(1)}, f32[2,6,6,1024]{3,2,1,0:T(8,128)S(1)}, u32[]{:S(2)}, u32[]{:S(2)}) collective-permute-start(f32[2,6,6,1024]{3,2,1,0:T(8,128)S(1)} %get-tuple-element.33), channel_id=1, source_target_pairs={{1,0},{2,1},{3,2},{4,3},{5,4},{6,5},{7,6},{8,7},{9,8},{10,9},{11,1... | collective-permute-start | bytes 884744 | tf_op jit(solution)/shard_map/ppermute | solution.py:23
  141.0 1.9 copy-start.10
  141.1 12.0 %copy-start.15 = (bf16[2,6,12,512]{3,2,1,0:T(8,128)(2,1)}, bf16[2,6,12,512]{3,2,1,0:T(8,128)(2,1)S(1)}, u32[]{:S(2)}) copy-start(bf16[2,6,12,512]{3,2,1,0:T(8,128)(2,1)S(1)} %copy.74) | copy-start | bytes 442372
  141.1 12.7 %copy-start.2 = (bf16[2,6,12,1024]{3,0,2,1:T(2,128)(2,1)S(1)}, bf16[2,6,12,1024]{3,0,2,1:T(2,128)(2,1)}, u32[]{:S(2)}) copy-start(bf16[2,6,12,1024]{3,0,2,1:T(2,128)(2,1)} %param.6) | copy-start | bytes 884740
  141.1 12.7 %copy-start.17 = (f32[1024]{0:T(1024)S(1)}, f32[1024]{0:T(1024)}, u32[]{:S(2)}) copy-start(f32[1024]{0:T(1024)} %param.7) | copy-start | bytes 12292
  141.1 12.7 %copy-start.18 = (f32[1024]{0:T(1024)S(1)}, f32[1024]{0:T(1024)}, u32[]{:S(2)}) copy-start(f32[1024]{0:T(1024)} %param.8) | copy-start | bytes 12292
  153.1 0.8 copy-start.13
  157.7 2.8 copy-start.14
  157.7 2.8 copy-start.16
  160.5 1.4 copy-start.7
Sparse Core Ops, SparseCore 0:
  157.8 282.6 all-reduce.11
where the time goes:
time: 454 us; the launch traced here: 450 us
  waiting for transfers between devices  202 us (44%)
  blocking collectives  84 us (19%)
  local copies, waits for them, and re-layouts  75.7 us (17%)
  matrix products  29.7 us (7%)
  other arithmetic  22.9 us (5%)
  starting transfers between devices  21.4 us (5%)
  between operations  14.5 us (3%)
    unnamed x2, waiting for transfers between devices  192 us
    unnamed x1, blocking collectives  84 us
    ppermute x4, starting transfers between devices, padded(): lax.ppermute(tail, axis, [(i, (i + 1) % count) for i in range(ends)])  12.8 us
  transfers between devices with their start and end apart: 9, of which 3 were waited for; matrix products, arithmetic and copies ran while one was open for 9% of the time, Pallas kernels for 0%

commit v1 on v0

v1 whole, which is shorter than its diff:
```python
import math

import jax
import jax.numpy as jnp
from jax import lax
from jax.experimental import pallas as pl
from jax.experimental.pallas import tpu as pltpu
from jax.sharding import PartitionSpec as P

MESH = pl.DeviceIdType.MESH
BF = jnp.bfloat16
F32 = jnp.float32

D = 1024
HD = 512
TOK = 144
QUARTER = 36
NX, NY, NZ = 4, 4, 8
LAT, LON = 16, 16
PHASES = 2
WIDTH = 1024


def dot(a, b):
    return jnp.dot(a, b, preferred_element_type=F32)


def dot_nt(a, b):
    return lax.dot_general(a, b, (((1,), (1,)), ((), ())), preferred_element_type=F32)


def dot_tn(a, b):
    return lax.dot_general(a, b, (((0,), (0,)), ((), ())), preferred_element_type=F32)


def kernel(
    norm_factor,
    tok_ref,
    cot_ref,
    gain_ref,
    bias_ref,
    wqkv_hbm,
    wout_hbm,
    y_ref,
    tg_ref,
    dqkv_ref,
    dout_ref,
    vec_ref,
    wqkv,
    wout,
    xin,
    cin,
    xhat_s,
    normed_t,
    cot_t,
    proj,
    gatt,
    att,
    grads,
    part,
    core_in,
    core_sum,
    xy_in,
    z_out,
    z_in,
    vec_s,
    vec_core,
    vec_xy,
    vec_z,
    ysend,
    tsend,
    local_sem,
    ex_send,
    ex_recv,
    core_send,
    core_recv,
    xy_send,
    xy_recv,
    z_send,
    z_recv,
):
    lat = lax.axis_index("lat")
    lon = lax.axis_index("lon")
    x_lo = lat // 8
    y = lax.rem(lat // 2, 4)
    core = lax.rem(lat, 2)
    x_hi = lon // 8
    z = lax.rem(lon, 8)
    x = x_hi * 2 + x_lo
    odd = core

    def wrap(v):
        return lax.rem(v + 16, 16)

    sibling = (lat + 1 - 2 * core, lon)
    plane = []
    for sx in range(NX):
        for sy in range(NY):
            if sx or sy:
                px = lax.rem(x + sx, NX)
                py = lax.rem(y + sy, NY)
                row = lax.rem(px, 2) * 4 + py
                plane.append(((row * 2 + core, (px // 2) * 8 + z), row, px // 2))
    column = []
    for s in range(1, NZ):
        pz = lax.rem(z + s, NZ)
        column.append(((lat, x_hi * 8 + pz), pz))

    send_to = [
        ((lat, wrap(lon + 1 - 2 * odd)), 0, 1 - odd, 2 + odd),
        ((wrap(lat + 1), wrap(lon - 1 + odd)), 1, 0, 1),
        ((wrap(lat + 1), wrap(lon + odd)), 1, 1, 0),
    ]
    give_back = [
        ((lat, wrap(lon - 1 + 2 * odd)), 0, 1 - odd, 2 + odd),
        ((wrap(lat - 1), wrap(lon + odd)), 1, 0, 1),
        ((wrap(lat - 1), wrap(lon - 1 + odd)), 1, 1, 0),
    ]

    load_wqkv = pltpu.make_async_copy(wqkv_hbm, wqkv, local_sem.at[0])
    load_wout = pltpu.make_async_copy(wout_hbm, wout, local_sem.at[1])

    barrier = pltpu.get_barrier_semaphore()
    friends = (
        [p[0] for p in send_to]
        + [p[0] for p in give_back]
        + [sibling]
        + [p[0] for p in plane]
        + [p[0] for p in column]
    )
    for peer in friends:
        pl.semaphore_signal(barrier, inc=1, device_id=peer, device_id_type=MESH)

    def quarter(ref, row_half, col_half):
        return ref.at[pl.ds(3 * row_half, 3), pl.ds(6 * col_half, 6)]

    own_x = pltpu.make_async_copy(quarter(tok_ref, 0, odd), xin.at[3 - odd], local_sem.at[2])
    own_c = pltpu.make_async_copy(quarter(cot_ref, 0, odd), cin.at[3 - odd], local_sem.at[3])
    own_x.start()
    load_wqkv.start()
    own_c.start()
    load_wout.start()
    pl.semaphore_wait(barrier, len(friends))

    enter = []
    for kind, (src, dst) in enumerate(((tok_ref, xin), (cot_ref, cin))):
        row = []
        for m, (peer, rh, ch, slot) in enumerate(send_to):
            copy = pltpu.make_async_remote_copy(
                src_ref=quarter(src, rh, ch),
                dst_ref=dst.at[slot],
                send_sem=ex_send.at[kind, m],
                recv_sem=ex_recv.at[kind, m],
                device_id=peer,
                device_id_type=MESH,
            )
            copy.start()
            row.append(copy)
        enter.append(row)

    own_x.wait()
    for copy in enter[0]:
        copy.wait_recv()
    tokens = xin[...].reshape(TOK, D).astype(F32)
    centered = tokens - jnp.mean(tokens, axis=-1, keepdims=True)
    inverse = lax.rsqrt(jnp.mean(centered * centered, axis=-1, keepdims=True) + 1e-05)
    xhat = centered * inverse
    xhat_s[...] = xhat
    normed = (xhat * gain_ref[...] + bias_ref[...]).astype(BF)
    load_wqkv.wait()
    proj[...] = dot(normed, wqkv[...]).astype(BF)
    normed_t[...] = normed.T
    own_c.wait()
    for copy in enter[1]:
        copy.wait_recv()
    load_wout.wait()
    cot = cin[...].reshape(TOK, D)
    gatt[...] = dot_nt(cot, wout[...]).astype(BF)
    cot_t[...] = cot.T

    slot_q = lax.broadcasted_iota(jnp.int32, (TOK, TOK), 0) // QUARTER
    slot_k = lax.broadcasted_iota(jnp.int32, (TOK, TOK), 1) // QUARTER
    lat_edge = (lat == 0).astype(jnp.int32)
    lon_edge = (lon == odd * (LON - 1)).astype(jnp.int32)
    apart = lat_edge * jnp.abs(slot_q // 2 - slot_k // 2) + lon_edge * jnp.abs(
        lax.rem(slot_q, 2) - lax.rem(slot_k, 2)
    )
    valid = apart == 0
    lane = lax.broadcasted_iota(jnp.int32, (TOK, 128), 1)
    low = lane < 64
    halves = (low.astype(F32).astype(BF), (1.0 - low.astype(F32)).astype(BF))
    probs = []
    for pair in range(4):
        at = slice(pair * 128, pair * 128 + 128)
        q2 = proj[:, at]
        k2 = proj[:, 512 + pair * 128 : 640 + pair * 128]
        v2 = proj[:, 1024 + pair * 128 : 1152 + pair * 128]
        g2 = gatt[:, at]
        mixed = []
        grad_v = []
        grad_q = []
        grad_k = []
        for half in halves:
            kh = k2 * half
            vh = v2 * half
            scores = jnp.where(valid, dot_nt(q2, kh) * 0.125, -1e30)
            top = jnp.max(scores, axis=-1, keepdims=True)
            e = jnp.exp(scores - top)
            p = e * (1.0 / jnp.sum(e, axis=-1, keepdims=True))
            p_low = p.astype(BF)
            mixed.append(dot(p_low, vh))
            grad_v.append(dot_tn(p_low, g2))
            gp = dot_nt(g2, vh)
            inner = jnp.sum(p * gp, axis=-1, keepdims=True)
            gs = (p * (gp - inner)).astype(BF)
            grad_q.append(dot(gs, kh))
            grad_k.append(dot_tn(gs, q2))
        att[:, at] = (mixed[0] + mixed[1]).astype(BF)
        grads[:, at] = ((grad_q[0] + grad_q[1]) * 0.125).astype(BF)
        grads[:, 512 + pair * 128 : 640 + pair * 128] = (
            jnp.where(low, grad_k[0], grad_k[1]) * 0.125
        ).astype(BF)
        grads[:, 1024 + pair * 128 : 1152 + pair * 128] = jnp.where(
            low, grad_v[0], grad_v[1]
        ).astype(BF)

    def store_part(phase, col, left, right):
        for block in range(4):
            rows = dot(left[block * 256 : block * 256 + 256, :], right).astype(BF)
            rows = rows.reshape(2, 2, 2, 32, 512)
            for t in range(2):
                for c in range(2):
                    part[phase, c, block * 2 + t, :, :, col : col + 512] = rows[t, c]

    def start_core(phase):
        copy = pltpu.make_async_remote_copy(
            src_ref=part.at[phase, 1 - core],
            dst_ref=core_in.at[phase],
            send_sem=core_send.at[phase],
            recv_sem=core_recv.at[phase],
            device_id=sibling,
            device_id_type=MESH,
        )
        copy.start()
        return copy

    def start_plane(phase):
        copies = []
        for n, (peer, row, hi) in enumerate(plane):
            copy = pltpu.make_async_remote_copy(
                src_ref=core_sum.at[phase, row, hi],
                dst_ref=xy_in.at[phase, n],
                send_sem=xy_send.at[phase, n],
                recv_sem=xy_recv.at[phase, n],
                device_id=peer,
                device_id_type=MESH,
            )
            copy.start()
            copies.append(copy)
        return copies

    def start_column(phase):
        copies = []
        for n, (peer, pz) in enumerate(column):
            copy = pltpu.make_async_remote_copy(
                src_ref=z_out.at[phase, pz],
                dst_ref=z_in.at[phase, n],
                send_sem=z_send.at[phase, n],
                recv_sem=z_recv.at[phase, n],
                device_id=peer,
                device_id_type=MESH,
            )
            copy.start()
            copies.append(copy)
        return copies

    def add_core(phase, copy):
        copy.wait_recv()
        for row in range(8):
            core_sum[phase, row] = (
                part[phase, core, row].astype(F32) + core_in[phase, row].astype(F32)
            ).astype(BF)

    store_part(0, 0, cot_t, att[...])
    store_part(0, 512, normed_t, grads[:, 1024:1536])
    core_0 = start_core(0)
    store_part(1, 0, normed_t, grads[:, 0:512])
    store_part(1, 512, normed_t, grads[:, 512:1024])
    core_1 = start_core(1)
    add_core(0, core_0)
    plane_0 = start_plane(0)
    gn = dot_nt(grads[...], wqkv[...])
    xh = xhat_s[...]
    vec_s[0:1, :] = jnp.sum(gn * xh, axis=0, keepdims=True)
    vec_s[1:2, :] = jnp.sum(gn, axis=0, keepdims=True)
    vec_1 = pltpu.make_async_remote_copy(
        src_ref=vec_s,
        dst_ref=vec_core,
        send_sem=core_send.at[2],
        recv_sem=core_recv.at[2],
        device_id=sibling,
        device_id_type=MESH,
    )
    vec_1.start()
    add_core(1, core_1)
    plane_1 = start_plane(1)

    gh = gn * gain_ref[...]
    first = jnp.mean(gh, axis=-1, keepdims=True)
    second = jnp.mean(gh * xh, axis=-1, keepdims=True)
    cot_wide = cin[...].reshape(TOK, D).astype(F32)
    tg = (cot_wide + (gh - first - xh * second) * inverse).astype(BF)
    tsend[...] = tg.reshape(4, 3, 6, 2, D)

    def start_back(kind, src, dst):
        copies = []
        for m, (peer, rh, ch, slot) in enumerate(give_back):
            copy = pltpu.make_async_remote_copy(
                src_ref=src.at[slot],
                dst_ref=quarter(dst, rh, ch),
                send_sem=ex_send.at[kind, m],
                recv_sem=ex_recv.at[kind, m],
                device_id=peer,
                device_id_type=MESH,
            )
            copy.start()
            copies.append(copy)
        own = pltpu.make_async_copy(src.at[3 - odd], quarter(dst, 0, odd), local_sem.at[2 + kind])
        own.start()
        return copies, own

    back_t, own_t = start_back(2, tsend, tg_ref)
    vec_1.wait_recv()
    vec_core[...] = vec_core[...] + vec_s[...]
    vec_2 = []
    for n, (peer, _, _) in enumerate(plane):
        copy = pltpu.make_async_remote_copy(
            src_ref=vec_core,
            dst_ref=vec_xy.at[n],
            send_sem=xy_send.at[2, n],
            recv_sem=xy_recv.at[2, n],
            device_id=peer,
            device_id_type=MESH,
        )
        copy.start()
        vec_2.append(copy)
    mixed_out = dot(att[...], wout[...])
    y_out = (xin[...].reshape(TOK, D).astype(F32) + mixed_out).astype(BF)
    ysend[...] = y_out.reshape(4, 3, 6, 2, D)
    back_y, own_y = start_back(3, ysend, y_ref)

    def add_plane(phase, copies):
        for copy in copies:
            copy.wait_recv()
        total = core_sum[phase, x_lo * 4 + y, x_hi].astype(F32)
        for n in range(len(copies)):
            total = total + xy_in[phase, n].astype(F32)
        z_out[phase] = total.astype(BF).reshape(8, 4, WIDTH)

    add_plane(0, plane_0)
    column_0 = start_column(0)
    for copy in vec_2:
        copy.wait_recv()
    vec_total = vec_core[...]
    for n in range(len(vec_2)):
        vec_total = vec_total + vec_xy[n]
    vec_s2 = vec_total
    vec_1.wait_send()
    vec_s[...] = vec_s2
    vec_3 = []
    for n, (peer, _) in enumerate(column):
        copy = pltpu.make_async_remote_copy(
            src_ref=vec_s,
            dst_ref=vec_z.at[n],
            send_sem=z_send.at[2, n],
            recv_sem=z_recv.at[2, n],
            device_id=peer,
            device_id_type=MESH,
        )
        copy.start()
        vec_3.append(copy)
    add_plane(1, plane_1)
    column_1 = start_column(1)

    def add_column(phase, copies):
        for copy in copies:
            copy.wait_recv()
        total = z_out[phase, z].astype(F32)
        for n in range(len(copies)):
            total = total + z_in[phase, n].astype(F32)
        return total * norm_factor

    done = add_column(0, column_0)
    dout_ref[...] = done[:, 0:512]
    dqkv_ref[:, 1024:1536] = done[:, 512:1024]
    for copy in vec_3:
        copy.wait_recv()
    vec_total = vec_s[...]
    for n in range(len(vec_3)):
        vec_total = vec_total + vec_z[n]
    place = lat * LON + lon
    for copy in vec_2:
        copy.wait_send()
    vec_core[...] = vec_total * norm_factor
    lanes = vec_core[:, pl.ds(pl.multiple_of((place // 32) * 128, 128), 128)]
    vec_ref[...] = pltpu.roll(lanes, 128 - 4 * lax.rem(place, 32), 1)
    done = add_column(1, column_1)
    dqkv_ref[:, 0:1024] = done
    for copy in back_t + back_y:
        copy.wait()
    own_t.wait()
    own_y.wait()
    for copy in enter[0] + enter[1] + plane_0 + plane_1 + column_0 + column_1 + vec_3:
        copy.wait_send()
    core_0.wait_send()
    core_1.wait_send()


def on_device(tokens, layer_norm_gain, layer_norm_bias, w_qkv, w_out, output_cotangent):
    total_tokens = tokens.shape[0] * tokens.shape[1] * tokens.shape[2] * LAT * LON
    norm_factor = 1.0 / math.sqrt(total_tokens)
    grid_shape = (6, 12, 2, D)
    anywhere = pl.BlockSpec(memory_space=pl.ANY)
    vmem = pl.BlockSpec(memory_space=pltpu.VMEM)
    dma = pltpu.SemaphoreType.DMA

    def body(*refs):
        kernel(norm_factor, *refs)

    y_out, token_gradient, d_qkv, d_out, vec = pl.pallas_call(
        body,
        out_shape=(
            jax.ShapeDtypeStruct(grid_shape, BF),
            jax.ShapeDtypeStruct(grid_shape, BF),
            jax.ShapeDtypeStruct((4, 1536), F32),
            jax.ShapeDtypeStruct((4, HD), F32),
            jax.ShapeDtypeStruct((2, 128), F32),
        ),
        in_specs=[anywhere, anywhere, vmem, vmem, anywhere, anywhere],
        out_specs=(anywhere, anywhere, vmem, vmem, vmem),
        scratch_shapes=[
            pltpu.VMEM((D, 1536), BF),
            pltpu.VMEM((HD, D), BF),
            pltpu.VMEM((4, 3, 6, 2, D), BF),
            pltpu.VMEM((4, 3, 6, 2, D), BF),
            pltpu.VMEM((TOK, D), F32),
            pltpu.VMEM((D, TOK), BF),
            pltpu.VMEM((D, TOK), BF),
            pltpu.VMEM((TOK, 1536), BF),
            pltpu.VMEM((TOK, HD), BF),
            pltpu.VMEM((TOK, HD), BF),
            pltpu.VMEM((TOK, 1536), BF),
            pltpu.VMEM((PHASES, 2, 8, 2, 32, WIDTH), BF),
            pltpu.VMEM((PHASES, 8, 2, 32, WIDTH), BF),
            pltpu.VMEM((PHASES, 8, 2, 32, WIDTH), BF),
            pltpu.VMEM((PHASES, 15, 32, WIDTH), BF),
            pltpu.VMEM((PHASES, 8, 4, WIDTH), BF),
            pltpu.VMEM((PHASES, 7, 4, WIDTH), BF),
            pltpu.VMEM((2, D), F32),
            pltpu.VMEM((2, D), F32),
            pltpu.VMEM((15, 2, D), F32),
            pltpu.VMEM((7, 2, D), F32),
            pltpu.VMEM((4, 3, 6, 2, D), BF),
            pltpu.VMEM((4, 3, 6, 2, D), BF),
            dma((6,)),
            dma((4, 3)),
            dma((4, 3)),
            dma((3,)),
            dma((3,)),
            dma((3, 15)),
            dma((3, 15)),
            dma((3, 7)),
            dma((3, 7)),
        ],
        compiler_params=pltpu.CompilerParams(
            collective_id=0, has_side_effects=True, vmem_limit_bytes=56 << 20
        ),
        name="window_step",
    )(
        tokens.transpose(1, 2, 0, 3),
        output_cotangent.transpose(1, 2, 0, 3),
        layer_norm_gain.reshape(1, D),
        layer_norm_bias.reshape(1, D),
        w_qkv,
        w_out,
    )
    return (
        y_out.transpose(2, 0, 1, 3),
        token_gradient.transpose(2, 0, 1, 3),
        d_qkv,
        d_out.T,
        vec[0, 0:4],
        vec[1, 0:4],
    )


def solution(mesh):
    in_specs = (P(None, "lat", "lon", None), P(), P(), P(), P(), P(None, "lat", "lon", None))
    out_specs = (
        P(None, "lat", "lon", None),
        P(None, "lat", "lon", None),
        P(("lat", "lon"), None),
        P(None, ("lat", "lon")),
        P(("lat", "lon")),
        P(("lat", "lon")),
    )
    return jax.shard_map(
        on_device, mesh=mesh, in_specs=in_specs, out_specs=out_specs, check_vma=False
    )
```

time: 454 us -> 73.1 us (0.16)
  the two profiles are of different devices: /device:TPU:32 before, /device:TPU:4 now
where the time goes in v1:
time: 73.1 us; the launch traced here: 72.8 us
  Pallas kernels  64.5 us (88%)
  local copies, waits for them, and re-layouts  7.65 us (10%)
    pallas_call x1, Pallas kernels, on_device(): pl.pallas_call(body, out_shape=(jax.ShapeDtypeStruct(grid_shape, BF), jax...  64.5 us
    unnamed x4, local copies, waits for them, and re-layouts  6.4 us

profile of v1, /device:TPU:4, one launch (start us, length us, event | category | flops | bytes accessed | tf_op | source)
XLA Modules:
  0.0 72.8 jit_solution(14119404386246732845)
XLA Ops:
  0.6 64.5 %window_step.1 = (bf16[6,12,2,1024]{3,2,1,0:T(2,128)(2,1)}, bf16[6,12,2,1024]{3,2,1,0:T(2,128)(2,1)}, f32[4,1536]{1,0:T(4,128)}, f32[4,512]{1,0:T(4,128)}, f32[2,128]{1,0:T(2,128)}) custom-call(bf16[6,12,2,1024]{3,2,1,0:T(2,128)(2,1)} %bitcast.11, bf16[6,12,2,1024]{3,2,1,0:T(2,128)(2,1)} %bitcast.12, f32[1,1024]{1,0:T(1,128)} %bitcast.16, ...), custom_call_target="tpu_custom_call" | custom-call | tf_op jit(solution)/shard_map/window_step/pallas_call | solution.py:430
  65.2 1.3 %slice_bitcast_fusion = (f32[4]{0:T(128)}, f32[4]{0:T(128)}) fusion(f32[2,128]{1,0:T(2,128)} %get-tuple-element.15), kind=kLoop, calls=%fused_computation | loop fusion | bytes 64 | tf_op jit(solution)/shard_map/squeeze | solution.py:493
  66.4 1.9 %copy.16 = bf16[2,6,12,1024]{3,0,2,1:T(2,128)(2,1)} copy(bf16[2,6,12,1024]{3,0,2,1:T(2,128)(2,1)} %bitcast.14) | data formatting | bytes 589824
  68.3 1.9 %copy.17 = bf16[2,6,12,1024]{3,0,2,1:T(2,128)(2,1)} copy(bf16[2,6,12,1024]{3,0,2,1:T(2,128)(2,1)} %bitcast.13) | data formatting | bytes 589824
  70.2 1.3 %copy.18 = f32[4,1536]{1,0:T(4,128)} copy(f32[4,1536]{1,0:T(4,128)} %get-tuple-element.26) | data formatting | bytes 49152
  71.5 1.3 %copy.19 = f32[512,4]{0,1:T(4,128)} copy(f32[512,4]{0,1:T(4,128)} %bitcast.15) | data formatting | bytes 16384

commit v2 on v1

v2 whole, which is shorter than its diff:
```python
import math

import jax
import jax.numpy as jnp
from jax import lax
from jax.experimental import pallas as pl
from jax.experimental.pallas import tpu as pltpu
from jax.sharding import PartitionSpec as P

MESH = pl.DeviceIdType.MESH
BF = jnp.bfloat16
F32 = jnp.float32

D = 1024
HD = 512
TOK = 144
QUARTER = 36
NX, NY, NZ = 4, 4, 8
LAT, LON = 16, 16


def dot(a, b):
    return jnp.dot(a, b, preferred_element_type=F32)


def dot_nt(a, b):
    return lax.dot_general(a, b, (((1,), (1,)), ((), ())), preferred_element_type=F32)


def dot_tn(a, b):
    return lax.dot_general(a, b, (((0,), (0,)), ((), ())), preferred_element_type=F32)


OUT, VAL, QUE, KEY = range(4)
X_FIRST = (OUT, QUE)


def kernel(
    norm_factor,
    tok_ref,
    cot_ref,
    gain_ref,
    bias_ref,
    wqkv_hbm,
    wout_hbm,
    y_ref,
    tg_ref,
    dqkv_ref,
    dout_ref,
    vec_ref,
    wqkv,
    wout,
    xin,
    cin,
    xhat_s,
    left,
    left_in,
    proj,
    gatt,
    probs,
    right,
    right_in,
    part,
    one_in,
    mid,
    two_in,
    z_out,
    z_in,
    vec_out,
    vec_core,
    vec_xy,
    vec_z,
    ysend,
    tsend,
    local_sem,
    ex_send,
    ex_recv,
    core_send,
    core_recv,
    one_send,
    one_recv,
    two_send,
    two_recv,
    z_send,
    z_recv,
    vec_send,
    vec_recv,
):
    lat = lax.axis_index("lat")
    lon = lax.axis_index("lon")
    x_lo = lat // 8
    y = lax.rem(lat // 2, 4)
    core = lax.rem(lat, 2)
    x_hi = lon // 8
    z = lax.rem(lon, 8)
    x = x_hi * 2 + x_lo
    odd = core

    def wrap(v):
        return lax.rem(v + 16, 16)

    sibling = (lat + 1 - 2 * core, lon)
    along_x = []
    for s in range(1, NX):
        px = lax.rem(x + s, NX)
        along_x.append(((lax.rem(px, 2) * 8 + y * 2 + core, (px // 2) * 8 + z), px))
    along_y = []
    for s in range(1, NY):
        py = lax.rem(y + s, NY)
        along_y.append((((x_lo * 4 + py) * 2 + core, lon), py))
    along_z = []
    for s in range(1, NZ):
        pz = lax.rem(z + s, NZ)
        along_z.append(((lat, x_hi * 8 + pz), pz))

    send_to = [
        ((lat, wrap(lon + 1 - 2 * odd)), 0, 1 - odd, 2 + odd),
        ((wrap(lat + 1), wrap(lon - 1 + odd)), 1, 0, 1),
        ((wrap(lat + 1), wrap(lon + odd)), 1, 1, 0),
    ]
    give_back = [
        ((lat, wrap(lon - 1 + 2 * odd)), 0, 1 - odd, 2 + odd),
        ((wrap(lat - 1), wrap(lon + odd)), 1, 0, 1),
        ((wrap(lat - 1), wrap(lon - 1 + odd)), 1, 1, 0),
    ]
    unsent = []

    def push(src, dst, send_sem, recv_sem, peer):
        copy = pltpu.make_async_remote_copy(
            src_ref=src,
            dst_ref=dst,
            send_sem=send_sem,
            recv_sem=recv_sem,
            device_id=peer,
            device_id_type=MESH,
        )
        copy.start()
        unsent.append(copy)
        return copy

    def arrived(copies):
        for copy in copies:
            copy.wait_recv()

    load_wqkv = pltpu.make_async_copy(wqkv_hbm, wqkv, local_sem.at[0])
    load_wout = pltpu.make_async_copy(wout_hbm, wout, local_sem.at[1])

    barrier = pltpu.get_barrier_semaphore()
    friends = [p[0] for p in along_z + along_x + along_y + send_to + give_back] + [sibling]
    for peer in friends:
        pl.semaphore_signal(barrier, inc=1, device_id=peer, device_id_type=MESH)

    def quarter(ref, row_half, col_half):
        return ref.at[pl.ds(3 * row_half, 3), pl.ds(6 * col_half, 6)]

    own_x = pltpu.make_async_copy(quarter(tok_ref, 0, odd), xin.at[3 - odd], local_sem.at[2])
    own_c = pltpu.make_async_copy(quarter(cot_ref, 0, odd), cin.at[3 - odd], local_sem.at[3])
    own_x.start()
    load_wqkv.start()
    own_c.start()
    load_wout.start()
    pl.semaphore_wait(barrier, len(friends))

    enter = []
    for kind, (src, dst) in enumerate(((tok_ref, xin), (cot_ref, cin))):
        enter.append(
            [
                push(
                    quarter(src, rh, ch),
                    dst.at[slot],
                    ex_send.at[kind, m],
                    ex_recv.at[kind, m],
                    peer,
                )
                for m, (peer, rh, ch, slot) in enumerate(send_to)
            ]
        )

    def share_left(kind, value):
        rows = value.reshape(8, 2, 64, TOK)
        for c in range(2):
            for t in range(8):
                left[kind, c, t] = rows[t, c]
        return push(
            left.at[kind, 1 - core],
            left_in.at[kind],
            core_send.at[kind],
            core_recv.at[kind],
            sibling,
        )

    own_x.wait()
    arrived(enter[0])
    tokens = xin[...].reshape(TOK, D).astype(F32)
    centered = tokens - jnp.mean(tokens, axis=-1, keepdims=True)
    inverse = lax.rsqrt(jnp.mean(centered * centered, axis=-1, keepdims=True) + 1e-05)
    xhat = centered * inverse
    xhat_s[...] = xhat
    normed = (xhat * gain_ref[...] + bias_ref[...]).astype(BF)
    load_wqkv.wait()
    proj[...] = dot(normed, wqkv[...]).astype(BF)
    left_n = share_left(0, normed.T)
    own_c.wait()
    arrived(enter[1])
    load_wout.wait()
    cot = cin[...].reshape(TOK, D)
    gatt[...] = dot_nt(cot, wout[...]).astype(BF)
    left_c = share_left(1, cot.T)

    slot_q = lax.broadcasted_iota(jnp.int32, (TOK, TOK), 0) // QUARTER
    slot_k = lax.broadcasted_iota(jnp.int32, (TOK, TOK), 1) // QUARTER
    lat_edge = (lat == 0).astype(jnp.int32)
    lon_edge = (lon == odd * (LON - 1)).astype(jnp.int32)
    apart = lat_edge * jnp.abs(slot_q // 2 - slot_k // 2) + lon_edge * jnp.abs(
        lax.rem(slot_q, 2) - lax.rem(slot_k, 2)
    )
    valid = apart == 0
    lane = lax.broadcasted_iota(jnp.int32, (TOK, 128), 1)
    low = lane < 64
    halves = (low.astype(F32).astype(BF), (1.0 - low.astype(F32)).astype(BF))

    def share_right(chunk):
        return push(
            right.at[chunk],
            right_in.at[chunk],
            core_send.at[2 + chunk],
            core_recv.at[2 + chunk],
            sibling,
        )

    for pair in range(4):
        at = slice(pair * 128, pair * 128 + 128)
        q2 = proj[:, at]
        k2 = proj[:, 512 + pair * 128 : 640 + pair * 128]
        v2 = proj[:, 1024 + pair * 128 : 1152 + pair * 128]
        g2 = gatt[:, at]
        mixed = []
        grad_v = []
        for h, half in enumerate(halves):
            scores = jnp.where(valid, dot_nt(q2, k2 * half) * 0.125, -1e30)
            top = jnp.max(scores, axis=-1, keepdims=True)
            e = jnp.exp(scores - top)
            p = e * (1.0 / jnp.sum(e, axis=-1, keepdims=True))
            probs[pair * 2 + h] = p
            p_low = p.astype(BF)
            mixed.append(dot(p_low, v2 * half))
            grad_v.append(dot_tn(p_low, g2))
        right[OUT, :, at] = (mixed[0] + mixed[1]).astype(BF)
        right[VAL, :, at] = jnp.where(low, grad_v[0], grad_v[1]).astype(BF)
    right_copies = [share_right(OUT), share_right(VAL)]
    for pair in range(4):
        at = slice(pair * 128, pair * 128 + 128)
        q2 = proj[:, at]
        k2 = proj[:, 512 + pair * 128 : 640 + pair * 128]
        v2 = proj[:, 1024 + pair * 128 : 1152 + pair * 128]
        g2 = gatt[:, at]
        grad_q = []
        grad_k = []
        for h, half in enumerate(halves):
            p = probs[pair * 2 + h]
            gp = dot_nt(g2, v2 * half)
            inner = jnp.sum(p * gp, axis=-1, keepdims=True)
            gs = (p * (gp - inner)).astype(BF)
            grad_q.append(dot(gs, k2 * half))
            grad_k.append(dot_tn(gs, q2))
        right[QUE, :, at] = ((grad_q[0] + grad_q[1]) * 0.125).astype(BF)
        right[KEY, :, at] = (jnp.where(low, grad_k[0], grad_k[1]) * 0.125).astype(BF)
    right_copies += [share_right(QUE), share_right(KEY)]

    def first_step(chunk):
        kind = 1 if chunk == OUT else 0
        x_first = chunk in X_FIRST
        right_copies[chunk].wait_recv()
        mine = right[chunk]
        other = right_in[chunk]
        for block in range(2):
            at = slice(block * 4, block * 4 + 4)
            rows = dot(left[kind, core, at].reshape(256, TOK), mine) + dot(
                left_in[kind, at].reshape(256, TOK), other
            )
            rows = rows.astype(BF).reshape(4, 2, 32, 512)
            for t in range(4):
                for hi in range(2):
                    gx = hi * 2 + block
                    if x_first:
                        part[chunk, gx, t] = rows[t, hi]
                    else:
                        part[chunk, t, gx] = rows[t, hi]
        return [
            push(
                part.at[chunk, place],
                one_in.at[chunk, n],
                one_send.at[chunk, n],
                one_recv.at[chunk, n],
                peer,
            )
            for n, (peer, place) in enumerate(along_x if x_first else along_y)
        ]

    def second_step(chunk, copies):
        x_first = chunk in X_FIRST
        arrived(copies)
        total = part[chunk, x if x_first else y].astype(F32)
        for n in range(3):
            total = total + one_in[chunk, n].astype(F32)
        mid[chunk] = total.astype(BF)
        return [
            push(
                mid.at[chunk, place],
                two_in.at[chunk, n],
                two_send.at[chunk, n],
                two_recv.at[chunk, n],
                peer,
            )
            for n, (peer, place) in enumerate(along_y if x_first else along_x)
        ]

    def third_step(phase, pair):
        for col, (chunk, copies) in enumerate(pair):
            arrived(copies)
            total = mid[chunk, y if chunk in X_FIRST else x].astype(F32)
            for n in range(3):
                total = total + two_in[chunk, n].astype(F32)
            z_out[phase, :, :, col * 512 : col * 512 + 512] = total.astype(BF).reshape(8, 4, 512)
        return [
            push(
                z_out.at[phase, place],
                z_in.at[phase, n],
                z_send.at[phase, n],
                z_recv.at[phase, n],
                peer,
            )
            for n, (peer, place) in enumerate(along_z)
        ]

    def last_step(phase, copies):
        arrived(copies)
        total = z_out[phase, z].astype(F32)
        for n in range(7):
            total = total + z_in[phase, n].astype(F32)
        return total * norm_factor

    def start_back(kind, src, dst):
        for m, (peer, rh, ch, slot) in enumerate(give_back):
            back.append(
                push(
                    src.at[slot],
                    quarter(dst, rh, ch),
                    ex_send.at[kind, m],
                    ex_recv.at[kind, m],
                    peer,
                )
            )
        own = pltpu.make_async_copy(src.at[3 - odd], quarter(dst, 0, odd), local_sem.at[2 + kind])
        own.start()
        return own

    back = []
    left_c.wait_recv()
    one_out = first_step(OUT)
    left_n.wait_recv()
    one_val = first_step(VAL)
    one_que = first_step(QUE)
    one_key = first_step(KEY)

    gn = dot_nt(right[QUE], wqkv[:, 0:512])
    gn = gn + dot_nt(right[KEY], wqkv[:, 512:1024])
    gn = gn + dot_nt(right[VAL], wqkv[:, 1024:1536])
    xh = xhat_s[...]
    vec_out[0, 0:1, :] = jnp.sum(gn * xh, axis=0, keepdims=True)
    vec_out[0, 1:2, :] = jnp.sum(gn, axis=0, keepdims=True)
    vec_0 = push(vec_out.at[0], vec_core, vec_send.at[0], vec_recv.at[0], sibling)
    gh = gn * gain_ref[...]
    first = jnp.mean(gh, axis=-1, keepdims=True)
    second = jnp.mean(gh * xh, axis=-1, keepdims=True)
    cot_wide = cin[...].reshape(TOK, D).astype(F32)
    tg = (cot_wide + (gh - first - xh * second) * inverse).astype(BF)
    tsend[...] = tg.reshape(4, 3, 6, 2, D)

    def vec_step(stage, total, peers, landing, first_sem):
        vec_out[stage] = total
        return [
            push(
                vec_out.at[stage],
                landing.at[n],
                vec_send.at[first_sem + n],
                vec_recv.at[first_sem + n],
                peer[0],
            )
            for n, peer in enumerate(peers)
        ]

    vec_0.wait_recv()
    vec_1 = vec_step(1, vec_out[0] + vec_core[...], along_x, vec_xy.at[0], 1)
    own_t = start_back(2, tsend, tg_ref)
    mixed_out = dot(right[OUT], wout[...])
    y_out = (xin[...].reshape(TOK, D).astype(F32) + mixed_out).astype(BF)
    ysend[...] = y_out.reshape(4, 3, 6, 2, D)
    own_y = start_back(3, ysend, y_ref)

    two_out = second_step(OUT, one_out)
    two_val = second_step(VAL, one_val)
    arrived(vec_1)
    total = vec_out[1]
    for n in range(3):
        total = total + vec_xy[0, n]
    vec_2 = vec_step(2, total, along_y, vec_xy.at[1], 4)
    two_que = second_step(QUE, one_que)
    two_key = second_step(KEY, one_key)
    z_first = third_step(0, ((OUT, two_out), (VAL, two_val)))
    arrived(vec_2)
    total = vec_out[2]
    for n in range(3):
        total = total + vec_xy[1, n]
    vec_3 = vec_step(3, total, along_z, vec_z, 7)
    z_second = third_step(1, ((QUE, two_que), (KEY, two_key)))

    done = last_step(0, z_first)
    dout_ref[...] = done[:, 0:512]
    dqkv_ref[:, 1024:1536] = done[:, 512:1024]
    arrived(vec_3)
    total = vec_out[3]
    for n in range(7):
        total = total + vec_z[n]
    place = lat * LON + lon
    vec_out[4] = total * norm_factor
    lanes = vec_out[4, :, pl.ds(pl.multiple_of((place // 32) * 128, 128), 128)]
    vec_ref[...] = pltpu.roll(lanes, 128 - 4 * lax.rem(place, 32), 1)
    done = last_step(1, z_second)
    dqkv_ref[:, 0:1024] = done
    arrived(back)
    own_t.wait()
    own_y.wait()
    for copy in unsent:
        copy.wait_send()


def finish(y_in, tg_in, dqkv_in, dout_in, vec_in, y_out, tg_out, dqkv_out, dout_out, gain_out, bias_out, sems):
    copies = [
        pltpu.make_async_copy(src, dst, sems.at[n])
        for n, (src, dst) in enumerate(
            ((y_in, y_out), (tg_in, tg_out), (dqkv_in, dqkv_out), (dout_in, dout_out))
        )
    ]
    for copy in copies:
        copy.start()
    gain_out[...] = vec_in[0:1, 0:4]
    bias_out[...] = vec_in[1:2, 0:4]
    for copy in copies:
        copy.wait()


def on_device(tokens, layer_norm_gain, layer_norm_bias, w_qkv, w_out, output_cotangent):
    total_tokens = tokens.shape[0] * tokens.shape[1] * tokens.shape[2] * LAT * LON
    norm_factor = 1.0 / math.sqrt(total_tokens)
    grid = jax.ShapeDtypeStruct((6, 12, 2, D), BF)
    d_qkv_shape = jax.ShapeDtypeStruct((4, 1536), F32)
    d_out_shape = jax.ShapeDtypeStruct((4, HD), F32)
    anywhere = pl.BlockSpec(memory_space=pl.ANY)
    vmem = pl.BlockSpec(memory_space=pltpu.VMEM)
    dma = pltpu.SemaphoreType.DMA

    def body(*refs):
        kernel(norm_factor, *refs)

    results = pl.pallas_call(
        body,
        out_shape=(
            pltpu.VMEM((6, 12, 2, D), BF),
            pltpu.VMEM((6, 12, 2, D), BF),
            pltpu.VMEM((4, 1536), F32),
            pltpu.VMEM((4, HD), F32),
            pltpu.VMEM((2, 128), F32),
        ),
        in_specs=[anywhere, anywhere, vmem, vmem, anywhere, anywhere],
        out_specs=(vmem,) * 5,
        scratch_shapes=[
            pltpu.VMEM((D, 1536), BF),
            pltpu.VMEM((HD, D), BF),
            pltpu.VMEM((4, 3, 6, 2, D), BF),
            pltpu.VMEM((4, 3, 6, 2, D), BF),
            pltpu.VMEM((TOK, D), F32),
            pltpu.VMEM((2, 2, 8, 64, TOK), BF),
            pltpu.VMEM((2, 8, 64, TOK), BF),
            pltpu.VMEM((TOK, 1536), BF),
            pltpu.VMEM((TOK, HD), BF),
            pltpu.VMEM((8, TOK, TOK), F32),
            pltpu.VMEM((4, TOK, HD), BF),
            pltpu.VMEM((4, TOK, HD), BF),
            pltpu.VMEM((4, 4, 4, 32, HD), BF),
            pltpu.VMEM((4, 3, 4, 32, HD), BF),
            pltpu.VMEM((4, 4, 32, HD), BF),
            pltpu.VMEM((4, 3, 32, HD), BF),
            pltpu.VMEM((2, 8, 4, 2 * HD), BF),
            pltpu.VMEM((2, 7, 4, 2 * HD), BF),
            pltpu.VMEM((5, 2, D), F32),
            pltpu.VMEM((2, D), F32),
            pltpu.VMEM((2, 3, 2, D), F32),
            pltpu.VMEM((7, 2, D), F32),
            pltpu.VMEM((4, 3, 6, 2, D), BF),
            pltpu.VMEM((4, 3, 6, 2, D), BF),
            dma((6,)),
            dma((4, 3)),
            dma((4, 3)),
            dma((6,)),
            dma((6,)),
            dma((4, 3)),
            dma((4, 3)),
            dma((4, 3)),
            dma((4, 3)),
            dma((2, 7)),
            dma((2, 7)),
            dma((14,)),
            dma((14,)),
        ],
        compiler_params=pltpu.CompilerParams(
            collective_id=0, has_side_effects=True, vmem_limit_bytes=56 << 20
        ),
        name="window_step",
    )(
        tokens.transpose(1, 2, 0, 3),
        output_cotangent.transpose(1, 2, 0, 3),
        layer_norm_gain.reshape(1, D),
        layer_norm_bias.reshape(1, D),
        w_qkv,
        w_out,
    )
    small = jax.ShapeDtypeStruct((1, 4), F32)
    y_out, token_gradient, d_qkv, d_out, gain_gradient, d_bias = pl.pallas_call(
        finish,
        out_shape=(grid, grid, d_qkv_shape, d_out_shape, small, small),
        in_specs=[vmem] * 5,
        out_specs=(anywhere, anywhere, anywhere, anywhere, vmem, vmem),
        scratch_shapes=[dma((4,))],
        name="hand_out",
    )(*[pltpu.with_memory_space_constraint(r, pltpu.VMEM) for r in results])
    return (
        y_out.transpose(2, 0, 1, 3),
        token_gradient.transpose(2, 0, 1, 3),
        d_qkv,
        d_out.T,
        gain_gradient.reshape(4),
        d_bias.reshape(4),
    )


def solution(mesh):
    in_specs = (P(None, "lat", "lon", None), P(), P(), P(), P(), P(None, "lat", "lon", None))
    out_specs = (
        P(None, "lat", "lon", None),
        P(None, "lat", "lon", None),
        P(("lat", "lon"), None),
        P(None, ("lat", "lon")),
        P(("lat", "lon")),
        P(("lat", "lon")),
    )
    return jax.shard_map(
        on_device, mesh=mesh, in_specs=in_specs, out_specs=out_specs, check_vma=False
    )
```

time: 73.1 us -> 51.6 us (0.71)
  the two profiles are of different devices: /device:TPU:4 before, /device:TPU:32 now
where the time goes in v2:
time: 51.6 us; the launch traced here: 51.5 us
  Pallas kernels  50.8 us (98%)
  between operations  0.64 us (1%)
    pallas_call x1, Pallas kernels, on_device(): pl.pallas_call(body, out_shape=(pltpu.VMEM((6, 12, 2, D), BF), pltpu.VMEM...  49.4 us
    pallas_call x1, Pallas kernels, on_device(): pl.pallas_call(finish, out_shape=(grid, grid, d_qkv_shape, d_out_shape, s...  1.37 us

profile of v2, /device:TPU:32, one launch (start us, length us, event | category | flops | bytes accessed | tf_op | source)
XLA Modules:
  0.0 51.5 jit_solution(7149844576882332810)
XLA Ops:
  0.6 49.4 %window_step.1 = (bf16[6,12,2,1024]{3,2,1,0:T(2,128)(2,1)S(1)}, bf16[6,12,2,1024]{3,2,1,0:T(2,128)(2,1)S(1)}, f32[4,1536]{1,0:T(4,128)S(1)}, f32[4,512]{1,0:T(4,128)S(1)}, f32[2,128]{1,0:T(2,128)S(1)}) custom-call(bf16[6,12,2,1024]{3,2,1,0:T(2,128)(2,1)} %bitcast.9, bf16[6,12,2,1024]{3,2,1,0:T(2,128)(2,1)} %bitcast.10, f32[1,1024]{1,0:T(1,128)} %bitcast.11, ...), custom_call_target="tpu_custom_call" | custom-call | tf_op jit(solution)/shard_map/window_step/pallas_call | solution.py:466
  50.1 1.4 %hand_out.1 = (bf16[6,12,2,1024]{3,2,1,0:T(2,128)(2,1)}, bf16[6,12,2,1024]{3,2,1,0:T(2,128)(2,1)}, f32[4,1536]{1,0:T(4,128)}, f32[4,512]{1,0:T(4,128)}, f32[1,4]{1,0:T(1,128)}, /*index=5*/f32[1,4]{1,0:T(1,128)}) custom-call(bf16[6,12,2,1024]{3,2,1,0:T(2,128)(2,1)S(1)} %get-tuple-element.17.y_in, bf16[6,12,2,1024]{3,2,1,0:T(2,128)(2,1)S(1)} %get-tuple-element.18.tg_in, ...), custom_call_target="tpu_custom_call" | custom-call | tf_op jit(solution)/shard_map/hand_out/pallas_call | solution.py:529

commit v3 on v2

--- a/solution.py
+++ b/solution.py
@@ -39,8 +39,8 @@
     norm_factor,
     tok_ref,
     cot_ref,
-    gain_ref,
-    bias_ref,
+    gain_hbm,
+    bias_hbm,
     wqkv_hbm,
     wout_hbm,
     y_ref,
@@ -48,6 +48,8 @@
     dqkv_ref,
     dout_ref,
     vec_ref,
+    gain_ref,
+    bias_ref,
     wqkv,
     wout,
     xin,
@@ -144,9 +146,11 @@
 
     load_wqkv = pltpu.make_async_copy(wqkv_hbm, wqkv, local_sem.at[0])
     load_wout = pltpu.make_async_copy(wout_hbm, wout, local_sem.at[1])
+    load_gain = pltpu.make_async_copy(gain_hbm, gain_ref, local_sem.at[6])
+    load_bias = pltpu.make_async_copy(bias_hbm, bias_ref, local_sem.at[7])
 
     barrier = pltpu.get_barrier_semaphore()
-    friends = [p[0] for p in along_z + along_x + along_y + send_to + give_back] + [sibling]
+    friends = [p[0] for p in send_to + give_back + along_z + along_x + along_y] + [sibling]
     for peer in friends:
         pl.semaphore_signal(barrier, inc=1, device_id=peer, device_id_type=MESH)
 
@@ -156,6 +160,8 @@
     own_x = pltpu.make_async_copy(quarter(tok_ref, 0, odd), xin.at[3 - odd], local_sem.at[2])
     own_c = pltpu.make_async_copy(quarter(cot_ref, 0, odd), cin.at[3 - odd], local_sem.at[3])
     own_x.start()
+    load_gain.start()
+    load_bias.start()
     load_wqkv.start()
     own_c.start()
     load_wout.start()
@@ -190,6 +196,8 @@
         )
 
     own_x.wait()
+    load_gain.wait()
+    load_bias.wait()
     arrived(enter[0])
     tokens = xin[...].reshape(TOK, D).astype(F32)
     centered = tokens - jnp.mean(tokens, axis=-1, keepdims=True)
@@ -199,13 +207,6 @@
     normed = (xhat * gain_ref[...] + bias_ref[...]).astype(BF)
     load_wqkv.wait()
     proj[...] = dot(normed, wqkv[...]).astype(BF)
-    left_n = share_left(0, normed.T)
-    own_c.wait()
-    arrived(enter[1])
-    load_wout.wait()
-    cot = cin[...].reshape(TOK, D)
-    gatt[...] = dot_nt(cot, wout[...]).astype(BF)
-    left_c = share_left(1, cot.T)
 
     slot_q = lax.broadcasted_iota(jnp.int32, (TOK, TOK), 0) // QUARTER
     slot_k = lax.broadcasted_iota(jnp.int32, (TOK, TOK), 1) // QUARTER
@@ -228,44 +229,45 @@
             sibling,
         )
 
-    for pair in range(4):
+    def columns(pair):
         at = slice(pair * 128, pair * 128 + 128)
         q2 = proj[:, at]
         k2 = proj[:, 512 + pair * 128 : 640 + pair * 128]
         v2 = proj[:, 1024 + pair * 128 : 1152 + pair * 128]
+        return at, q2, k2, v2
+
+    def forward(pair):
+        at, q2, k2, v2 = columns(pair)
+        mixed = []
+        for h, half in enumerate(halves):
+            scores = jnp.where(valid, dot_nt(k2 * half, q2) * 0.125, -1e30)
+            top = jnp.max(scores, axis=0, keepdims=True)
+            e = jnp.exp(scores - top)
+            p = e * (1.0 / jnp.sum(e, axis=0, keepdims=True))
+            probs[pair * 2 + h] = p
+            mixed.append(dot_tn(p.astype(BF), v2 * half))
+        right[OUT, :, at] = (mixed[0] + mixed[1]).astype(BF)
+
+    def value_gradient(pair):
+        at = slice(pair * 128, pair * 128 + 128)
         g2 = gatt[:, at]
-        mixed = []
-        grad_v = []
-        for h, half in enumerate(halves):
-            scores = jnp.where(valid, dot_nt(q2, k2 * half) * 0.125, -1e30)
-            top = jnp.max(scores, axis=-1, keepdims=True)
-            e = jnp.exp(scores - top)
-            p = e * (1.0 / jnp.sum(e, axis=-1, keepdims=True))
-            probs[pair * 2 + h] = p
-            p_low = p.astype(BF)
-            mixed.append(dot(p_low, v2 * half))
-            grad_v.append(dot_tn(p_low, g2))
-        right[OUT, :, at] = (mixed[0] + mixed[1]).astype(BF)
+        grad_v = [dot(probs[pair * 2 + h].astype(BF), g2) for h in range(2)]
         right[VAL, :, at] = jnp.where(low, grad_v[0], grad_v[1]).astype(BF)
-    right_copies = [share_right(OUT), share_right(VAL)]
-    for pair in range(4):
-        at = slice(pair * 128, pair * 128 + 128)
-        q2 = proj[:, at]
-        k2 = proj[:, 512 + pair * 128 : 640 + pair * 128]
-        v2 = proj[:, 1024 + pair * 128 : 1152 + pair * 128]
+
+    def backward(pair):
+        at, q2, k2, v2 = columns(pair)
         g2 = gatt[:, at]
         grad_q = []
         grad_k = []
         for h, half in enumerate(halves):
             p = probs[pair * 2 + h]
-            gp = dot_nt(g2, v2 * half)
-            inner = jnp.sum(p * gp, axis=-1, keepdims=True)
+            gp = dot_nt(v2 * half, g2)
+            inner = jnp.sum(p * gp, axis=0, keepdims=True)
             gs = (p * (gp - inner)).astype(BF)
-            grad_q.append(dot(gs, k2 * half))
-            grad_k.append(dot_tn(gs, q2))
+            grad_q.append(dot_tn(gs, k2 * half))
+            grad_k.append(dot(gs, q2))
         right[QUE, :, at] = ((grad_q[0] + grad_q[1]) * 0.125).astype(BF)
         right[KEY, :, at] = (jnp.where(low, grad_k[0], grad_k[1]) * 0.125).astype(BF)
-    right_copies += [share_right(QUE), share_right(KEY)]
 
     def first_step(chunk):
         kind = 1 if chunk == OUT else 0
@@ -356,12 +358,32 @@
         return own
 
     back = []
+    for pair in range(4):
+        forward(pair)
+    right_copies = [share_right(OUT)]
+    own_c.wait()
+    arrived(enter[1])
+    load_wout.wait()
+    cot = cin[...].reshape(TOK, D)
+    left_c = share_left(1, cot.T)
+    gatt[...] = dot_nt(cot, wout[...]).astype(BF)
+    for pair in range(4):
+        value_gradient(pair)
+    right_copies.append(share_right(VAL))
+    left_n = share_left(0, normed.T)
+    mixed_out = dot(right[OUT], wout[...])
+    y_out = (xin[...].reshape(TOK, D).astype(F32) + mixed_out).astype(BF)
+    ysend[...] = y_out.reshape(4, 3, 6, 2, D)
+    own_y = start_back(3, ysend, y_ref)
     left_c.wait_recv()
     one_out = first_step(OUT)
     left_n.wait_recv()
     one_val = first_step(VAL)
-    one_que = first_step(QUE)
-    one_key = first_step(KEY)
+    backward(0)
+    backward(1)
+    backward(2)
+    backward(3)
+    right_copies += [share_right(QUE), share_right(KEY)]
 
     gn = dot_nt(right[QUE], wqkv[:, 0:512])
     gn = gn + dot_nt(right[KEY], wqkv[:, 512:1024])
@@ -370,6 +392,8 @@
     vec_out[0, 0:1, :] = jnp.sum(gn * xh, axis=0, keepdims=True)
     vec_out[0, 1:2, :] = jnp.sum(gn, axis=0, keepdims=True)
     vec_0 = push(vec_out.at[0], vec_core, vec_send.at[0], vec_recv.at[0], sibling)
+    one_que = first_step(QUE)
+    one_key = first_step(KEY)
     gh = gn * gain_ref[...]
     first = jnp.mean(gh, axis=-1, keepdims=True)
     second = jnp.mean(gh * xh, axis=-1, keepdims=True)
@@ -392,11 +416,6 @@
 
     vec_0.wait_recv()
     vec_1 = vec_step(1, vec_out[0] + vec_core[...], along_x, vec_xy.at[0], 1)
-    own_t = start_back(2, tsend, tg_ref)
-    mixed_out = dot(right[OUT], wout[...])
-    y_out = (xin[...].reshape(TOK, D).astype(F32) + mixed_out).astype(BF)
-    ysend[...] = y_out.reshape(4, 3, 6, 2, D)
-    own_y = start_back(3, ysend, y_ref)
 
     two_out = second_step(OUT, one_out)
     two_val = second_step(VAL, one_val)
@@ -407,6 +426,7 @@
     vec_2 = vec_step(2, total, along_y, vec_xy.at[1], 4)
     two_que = second_step(QUE, one_que)
     two_key = second_step(KEY, one_key)
+    own_t = start_back(2, tsend, tg_ref)
     z_first = third_step(0, ((OUT, two_out), (VAL, two_val)))
     arrived(vec_2)
     total = vec_out[2]
@@ -415,6 +435,12 @@
     vec_3 = vec_step(3, total, along_z, vec_z, 7)
     z_second = third_step(1, ((QUE, two_que), (KEY, two_key)))
 
+    last_sends = z_second + vec_3
+    for copy in unsent[: len(unsent) - len(last_sends)]:
+        copy.wait_send()
+    arrived(back)
+    own_t.wait()
+    own_y.wait()
     done = last_step(0, z_first)
     dout_ref[...] = done[:, 0:512]
     dqkv_ref[:, 1024:1536] = done[:, 512:1024]
@@ -428,10 +454,7 @@
     vec_ref[...] = pltpu.roll(lanes, 128 - 4 * lax.rem(place, 32), 1)
     done = last_step(1, z_second)
     dqkv_ref[:, 0:1024] = done
-    arrived(back)
-    own_t.wait()
-    own_y.wait()
-    for copy in unsent:
+    for copy in last_sends:
         copy.wait_send()
 
 
@@ -472,9 +495,11 @@
             pltpu.VMEM((4, HD), F32),
             pltpu.VMEM((2, 128), F32),
         ),
-        in_specs=[anywhere, anywhere, vmem, vmem, anywhere, anywhere],
+        in_specs=[anywhere] * 6,
         out_specs=(vmem,) * 5,
         scratch_shapes=[
+            pltpu.VMEM((1, D), F32),
+            pltpu.VMEM((1, D), F32),
             pltpu.VMEM((D, 1536), BF),
             pltpu.VMEM((HD, D), BF),
             pltpu.VMEM((4, 3, 6, 2, D), BF),
@@ -499,7 +524,7 @@
             pltpu.VMEM((7, 2, D), F32),
             pltpu.VMEM((4, 3, 6, 2, D), BF),
             pltpu.VMEM((4, 3, 6, 2, D), BF),
-            dma((6,)),
+            dma((8,)),
             dma((4, 3)),
             dma((4, 3)),
             dma((6,)),

time: 51.6 us -> 48 us (0.930)
  Pallas kernels: 50.8 us -> 47.3 us
    pallas_call x1, Pallas kernels: 49.4 us -> 45.9 us  [on_device(): pl.pallas_call(body, out_shape=(pltpu.VMEM((6, 12, 2, D), BF), pltpu.VMEM...]
where the time goes in v3:
time: 48 us; the launch traced here: 47.9 us
  Pallas kernels  47.3 us (99%)
  between operations  0.64 us (1%)
    pallas_call x1, Pallas kernels, on_device(): pl.pallas_call(body, out_shape=(pltpu.VMEM((6, 12, 2, D), BF), pltpu.VMEM...  45.9 us
    pallas_call x1, Pallas kernels, on_device(): pl.pallas_call(finish, out_shape=(grid, grid, d_qkv_shape, d_out_shape, s...  1.37 us

profile of v3, /device:TPU:32, one launch (start us, length us, event | category | flops | bytes accessed | tf_op | source)
XLA Modules:
  0.0 47.9 jit_solution(16470512727394044949)
XLA Ops:
  0.6 45.9 %window_step.1 = (bf16[6,12,2,1024]{3,2,1,0:T(2,128)(2,1)S(1)}, bf16[6,12,2,1024]{3,2,1,0:T(2,128)(2,1)S(1)}, f32[4,1536]{1,0:T(4,128)S(1)}, f32[4,512]{1,0:T(4,128)S(1)}, f32[2,128]{1,0:T(2,128)S(1)}) custom-call(bf16[6,12,2,1024]{3,2,1,0:T(2,128)(2,1)} %bitcast.9, bf16[6,12,2,1024]{3,2,1,0:T(2,128)(2,1)} %bitcast.10, f32[1,1024]{1,0:T(1,128)} %bitcast.11, ...), custom_call_target="tpu_custom_call" | custom-call | tf_op jit(solution)/shard_map/window_step/pallas_call | solution.py:489
  46.6 1.4 %hand_out.1 = (bf16[6,12,2,1024]{3,2,1,0:T(2,128)(2,1)}, bf16[6,12,2,1024]{3,2,1,0:T(2,128)(2,1)}, f32[4,1536]{1,0:T(4,128)}, f32[4,512]{1,0:T(4,128)}, f32[1,4]{1,0:T(1,128)}, /*index=5*/f32[1,4]{1,0:T(1,128)}) custom-call(bf16[6,12,2,1024]{3,2,1,0:T(2,128)(2,1)S(1)} %get-tuple-element.17.y_in, bf16[6,12,2,1024]{3,2,1,0:T(2,128)(2,1)S(1)} %get-tuple-element.18.tg_in, ...), custom_call_target="tpu_custom_call" | custom-call | tf_op jit(solution)/shard_map/hand_out/pallas_call | solution.py:554

commit v4 on v3

--- a/solution.py
+++ b/solution.py
@@ -103,27 +103,27 @@
 
     sibling = (lat + 1 - 2 * core, lon)
     along_x = []
-    for s in range(1, NX):
+    for s in (2, 1, 3):
         px = lax.rem(x + s, NX)
         along_x.append(((lax.rem(px, 2) * 8 + y * 2 + core, (px // 2) * 8 + z), px))
     along_y = []
-    for s in range(1, NY):
+    for s in (2, 1, 3):
         py = lax.rem(y + s, NY)
         along_y.append((((x_lo * 4 + py) * 2 + core, lon), py))
     along_z = []
-    for s in range(1, NZ):
+    for s in (4, 3, 5, 2, 6, 1, 7):
         pz = lax.rem(z + s, NZ)
         along_z.append(((lat, x_hi * 8 + pz), pz))
 
     send_to = [
+        ((wrap(lat + 1), wrap(lon + odd)), 1, 1, 0),
+        ((wrap(lat + 1), wrap(lon - 1 + odd)), 1, 0, 1),
         ((lat, wrap(lon + 1 - 2 * odd)), 0, 1 - odd, 2 + odd),
-        ((wrap(lat + 1), wrap(lon - 1 + odd)), 1, 0, 1),
-        ((wrap(lat + 1), wrap(lon + odd)), 1, 1, 0),
     ]
     give_back = [
+        ((wrap(lat - 1), wrap(lon - 1 + odd)), 1, 1, 0),
+        ((wrap(lat - 1), wrap(lon + odd)), 1, 0, 1),
         ((lat, wrap(lon - 1 + 2 * odd)), 0, 1 - odd, 2 + odd),
-        ((wrap(lat - 1), wrap(lon + odd)), 1, 0, 1),
-        ((wrap(lat - 1), wrap(lon - 1 + odd)), 1, 1, 0),
     ]
     unsent = []
 
@@ -419,13 +419,13 @@
 
     two_out = second_step(OUT, one_out)
     two_val = second_step(VAL, one_val)
+    two_que = second_step(QUE, one_que)
+    two_key = second_step(KEY, one_key)
     arrived(vec_1)
     total = vec_out[1]
     for n in range(3):
         total = total + vec_xy[0, n]
     vec_2 = vec_step(2, total, along_y, vec_xy.at[1], 4)
-    two_que = second_step(QUE, one_que)
-    two_key = second_step(KEY, one_key)
     own_t = start_back(2, tsend, tg_ref)
     z_first = third_step(0, ((OUT, two_out), (VAL, two_val)))
     arrived(vec_2)

time: 48 us -> 47.3 us (0.985)
  Pallas kernels: 47.3 us -> 46.3 us
    pallas_call x1, Pallas kernels: 45.9 us -> 44.9 us  [on_device(): pl.pallas_call(body, out_shape=(pltpu.VMEM((6, 12, 2, D), BF), pltpu.VMEM...]
where the time goes in v4:
time: 47.3 us; the launch traced here: 46.9 us
  Pallas kernels  46.3 us (98%)
  between operations  0.64 us (1%)
    pallas_call x1, Pallas kernels, on_device(): pl.pallas_call(body, out_shape=(pltpu.VMEM((6, 12, 2, D), BF), pltpu.VMEM...  44.9 us
    pallas_call x1, Pallas kernels, on_device(): pl.pallas_call(finish, out_shape=(grid, grid, d_qkv_shape, d_out_shape, s...  1.37 us

profile of v4, /device:TPU:32, one launch (start us, length us, event | category | flops | bytes accessed | tf_op | source)
XLA Modules:
  0.0 46.9 jit_solution(12391935465711622761)
XLA Ops:
  0.6 44.9 %window_step.1 = (bf16[6,12,2,1024]{3,2,1,0:T(2,128)(2,1)S(1)}, bf16[6,12,2,1024]{3,2,1,0:T(2,128)(2,1)S(1)}, f32[4,1536]{1,0:T(4,128)S(1)}, f32[4,512]{1,0:T(4,128)S(1)}, f32[2,128]{1,0:T(2,128)S(1)}) custom-call(bf16[6,12,2,1024]{3,2,1,0:T(2,128)(2,1)} %bitcast.9, bf16[6,12,2,1024]{3,2,1,0:T(2,128)(2,1)} %bitcast.10, f32[1,1024]{1,0:T(1,128)} %bitcast.11, ...), custom_call_target="tpu_custom_call" | custom-call | tf_op jit(solution)/shard_map/window_step/pallas_call | solution.py:489
  45.6 1.4 %hand_out.1 = (bf16[6,12,2,1024]{3,2,1,0:T(2,128)(2,1)}, bf16[6,12,2,1024]{3,2,1,0:T(2,128)(2,1)}, f32[4,1536]{1,0:T(4,128)}, f32[4,512]{1,0:T(4,128)}, f32[1,4]{1,0:T(1,128)}, /*index=5*/f32[1,4]{1,0:T(1,128)}) custom-call(bf16[6,12,2,1024]{3,2,1,0:T(2,128)(2,1)S(1)} %get-tuple-element.17.y_in, bf16[6,12,2,1024]{3,2,1,0:T(2,128)(2,1)S(1)} %get-tuple-element.18.tg_in, ...), custom_call_target="tpu_custom_call" | custom-call | tf_op jit(solution)/shard_map/hand_out/pallas_call | solution.py:554
